TPU v7x, 256 devices: a whole 4x4x8 slice. The times are simulated.
256 devices in a mesh: lat: 64 (over x, y_lo, z), dp: 4 (over y_hi, core).
Axes of the slice: x: 4, y: 4 (y_hi: 2, y_lo: 2; y = y_hi * 2 + y_lo), z: 8, core: 2. Of those that a mesh axis runs over, the one named last changes fastest.
Arguments:
- inputs: bfloat16 [2048, 4096], P('dp', 'lat'), may hold values from -6 to 6
- dec_bias: bfloat16 [4096], P('lat'), may hold values from -3 to 3
- enc_weight: bfloat16 [4096, 16384], P(None, 'lat'), may hold values from -0.09375 to 0.09375
- enc_bias: float32 [16384], P('lat'), may hold values from -3 to 3
- dec_weight: bfloat16 [16384, 4096], P('lat'), may hold values from -0.046875 to 0.046875
- other_recon: float32 [2048, 4096], P('dp', 'lat'), may hold values from -6 to 6
- active_blocks: int32 [2048, 128], P('dp', 'lat'), may hold values 0 or 1
Outputs:
- error_full: float32 [2048, 4096], P('dp', 'lat')
- mse_loss: float32 [], replicated
- grad_dec: float32 [16384, 4096], P(('lat', 'dp'))
- grad_enc: float32 [4096, 16384], P(None, ('lat', 'dp'))
All inputs are finite; a program needn't handle non-finite values. No bound on the sum of `active_blocks` on one device may be relied on, other than what follows from the above.
Results may differ from a plain program's by a relative error of at most 0.0033.
Values may be sent and summed in bfloat16 or wider, within the bound.
A program may use at most 128 MiB of HBM per device.

v0:
```python
import jax
import jax.numpy as jnp
from jax import lax
from jax.sharding import PartitionSpec as P


def local(inputs, dec_bias, enc_weight, enc_bias, dec_weight, other_recon, active_blocks):
    row_count = inputs.shape[0]
    col_count = inputs.shape[1]
    block_size = enc_weight.shape[1] // active_blocks.shape[1]
    full_inputs, full_bias = (
        lax.all_gather(inputs, "lat", axis=1, tiled=True),
        lax.all_gather(dec_bias.reshape(1, -1), "lat", axis=1, tiled=True),
    )
    inputs_float = full_inputs.astype(jnp.float32)
    centered = (inputs_float - full_bias.astype(jnp.float32)).astype(jnp.bfloat16)
    pre_act = jnp.dot(centered, enc_weight, preferred_element_type=jnp.float32) + enc_bias[None, :]
    block_gate = (
        active_blocks.astype(jnp.float32)[:, :, None] * jnp.ones((1, 1, block_size), jnp.float32)
    ).reshape(row_count, -1)
    positive = jnp.maximum(pre_act, 0.0)
    activations = (positive * positive * block_gate).astype(jnp.bfloat16)
    outside = other_recon + dec_bias.astype(jnp.float32)[None, :]
    summed = lax.psum_scatter(
        lax.dot_general(
            dec_weight, activations, (((0,), (1,)), ((), ())), preferred_element_type=jnp.float32
        ),
        "lat",
        scatter_dimension=0,
        tiled=True,
    )
    error_local = summed.T + outside - inputs.astype(jnp.float32)
    error_bf = lax.all_gather(error_local.astype(jnp.bfloat16), "lat", axis=1, tiled=True)
    squares = lax.psum(jnp.sum(error_local * error_local), ("lat", "dp"))
    mse_loss = squares / (row_count * lax.axis_size("dp") * col_count * lax.axis_size("lat"))
    grad_dec = lax.psum_scatter(
        lax.dot_general(
            activations, error_bf, (((0,), (0,)), ((), ())), preferred_element_type=jnp.float32
        ),
        "dp",
        scatter_dimension=0,
        tiled=True,
    )
    dact = lax.dot_general(
        error_bf, dec_weight, (((1,), (1,)), ((), ())), preferred_element_type=jnp.float32
    )
    dpre = (dact * 2.0 * positive * block_gate).astype(jnp.bfloat16)
    enc_term = lax.dot_general(
        centered, dpre, (((0,), (0,)), ((), ())), preferred_element_type=jnp.float32
    )
    grad_enc = lax.psum_scatter(enc_term, "dp", scatter_dimension=1, tiled=True)
    return (error_local, mse_loss, grad_dec, grad_enc)


def solution(mesh):
    placed = (
        P("dp", "lat"),
        P("lat"),
        P(None, "lat"),
        P("lat"),
        P("lat", None),
        P("dp", "lat"),
        P("dp", "lat"),
    )
    return jax.shard_map(
        local,
        mesh=mesh,
        in_specs=placed,
        out_specs=(P("dp", "lat"), P(), P(("lat", "dp"), None), P(None, ("lat", "dp"))),
        check_vma=False,
    )
```

profile of v0, /device:TPU:1, one launch (start us, length us, event | category | flops | bytes accessed | tf_op | source)
XLA Modules:
  0.0 1096.9 jit_solution(8180831337322198771)
XLA Ops:
  7.2 0.0 copy-start
  7.2 0.0 all-gather.4.cloned.1.call-start
  7.2 0.7 all-gather.4.cloned.1.call-update
  7.9 0.0 reduce-scatter.10.cloned.1.call-start
  8.0 0.7 convert_element_type.27
  8.7 0.1 copy.15
  8.8 1.3 dynamic-slice
  10.8 0.9 dynamic-update-slice
  11.6 139.7 %all-reduce = bf16[4096]{0:T(1024)(128)(2,1)S(1)} all-reduce(bf16[4096]{0:T(1024)(128)(2,1)S(1)} %dynamic-update-slice), channel_id=2, replica_groups=mesh['lat'=64,'dp'=4] {'lat'}, use_global_device_ids=true, to_apply=%add | all-reduce | flops 4096 | bytes 16384
  151.4 123.1 %all-gather.4.cloned.1.call-done = bf16[512,4096]{0,1:T(8,128)(2,1)} async-done(((bf16[512,64]{0,1:T(8,128)(2,1)}), bf16[512,4096]{0,1:T(8,128)(2,1)}) %all-gather.4.cloned.1.call-update) | async-done | bytes 4194320 | tf_op jit(solution)/shard_map/all_gather | solution.py:12
  274.5 0.6 mul.27
  275.1 0.0 copy-start.1
  275.1 5.8 fusion.8
  280.8 0.0 copy-done.1
  280.8 0.0 copy-done
  280.8 4.5 convolution_bitcast_fusion
  285.3 9.0 copy.20
  294.3 0.0 copy-start.2
  294.3 0.0 copy-start.4
  294.3 0.0 copy-start.3
  294.3 0.0 reduce-scatter.10.cloned.1.call-update
  294.4 0.0 all-gather.6.cloned.1.call-start
  294.4 0.8 copy-done.2
  295.2 0.1 copy.17
  295.3 0.0 copy-done.4
  295.3 0.0 copy-done.3
  295.3 0.1 copy.16
  295.5 324.6 %reduce-scatter.10.cloned.1.call-done = f32[64,512]{1,0:T(8,128)} async-done(((f32[4096,512]{1,0:T(8,128)}), f32[64,512]{1,0:T(8,128)}) %reduce-scatter.10.cloned.1.call-update) | async-done | bytes 131088
  620.1 1.0 copy.21
  621.2 0.7 copy.18
  621.9 0.0 all-gather.6.cloned.1.call-update
  621.9 0.0 reduce-scatter.8.cloned.1.call-start
  622.0 300.7 %all-gather.6.cloned.1.call-done = bf16[512,4096]{0,1:T(8,128)(2,1)} async-done(((bf16[512,64]{0,1:T(8,128)(2,1)}), bf16[512,4096]{0,1:T(8,128)(2,1)}) %all-gather.6.cloned.1.call-update) | async-done | bytes 4194320 | tf_op jit(solution)/shard_map/all_gather | solution.py:33
  922.7 10.2 fusion
  932.9 0.0 reduce-scatter.8.cloned.1.call-update
  932.9 0.0 reduce-scatter.6.cloned.1.call-start
  933.0 5.4 fusion.15
  938.4 0.0 reduce-scatter.6.cloned.1.call-update
  938.5 0.7 multiply_reduce_fusion
  939.1 117.6 %psum.7 = f32[]{:T(128)} all-reduce(f32[]{:T(128)} %multiply_reduce_fusion), channel_id=1, replica_groups=mesh['lat'=64,'dp'=4] {'lat','dp'}, use_global_device_ids=true, to_apply=%region_2.0 | all-reduce | flops 1 | bytes 8 | tf_op jit(solution)/shard_map/psum | solution.py:34
  1056.8 0.8 copy.19
  1058.2 0.0 reduce-scatter.8.cloned.1.call-done
  1058.2 31.0 %reduce-scatter.6.cloned.1.call-done = f32[64,4096]{1,0:T(8,128)} async-done(((f32[256,4096]{1,0:T(8,128)}), f32[64,4096]{1,0:T(8,128)}) %reduce-scatter.6.cloned.1.call-update) | async-done | bytes 1048592 | tf_op jit(solution)/shard_map/reduce_scatter | solution.py:36
  (4 shorter events, 0.1 us)
Async XLA Ops:
  7.2 273.7 %copy-start = (bf16[256,4096]{1,0:T(8,128)(2,1)S(1)}, bf16[256,4096]{1,0:T(8,128)(2,1)}, u32[]{:S(2)}) copy-start(bf16[256,4096]{1,0:T(8,128)(2,1)} %param.11) | copy-start | bytes 6291460
  7.2 267.3 %all-gather.4.cloned.1.call-start = ((), (), s32[]{:S(2)}) async-start(), calls=%async_computation.3 | async-start | bytes 4259840 | tf_op jit(solution)/shard_map/all_gather | solution.py:12
  7.9 612.2 %reduce-scatter.10.cloned.1.call-start = ((), (), s32[]{:S(2)}) async-start(), calls=%async_computation.7 | async-start | bytes 8519680
  275.1 5.8 copy-start.1
  294.3 0.8 copy-start.2
  294.3 1.0 copy-start.4
  294.3 1.0 copy-start.3
  294.4 628.3 %all-gather.6.cloned.1.call-start = ((), (), s32[]{:S(2)}) async-start(), calls=%async_computation.4 | async-start | bytes 4259840 | tf_op jit(solution)/shard_map/all_gather | solution.py:33
  621.9 436.3 %reduce-scatter.8.cloned.1.call-start = ((), (), s32[]{:S(2)}) async-start(), calls=%async_computation.6 | async-start | bytes 5242880 | tf_op jit(solution)/shard_map/reduce_scatter | solution.py:51
  932.9 156.3 %reduce-scatter.6.cloned.1.call-start = ((), (), s32[]{:S(2)}) async-start(), calls=%async_computation.5 | async-start | bytes 5242880 | tf_op jit(solution)/shard_map/reduce_scatter | solution.py:36
Sparse Core Ops, SparseCore 0:
  9.8 264.6 all-gather.3
  294.5 325.5 reduce-scatter.9
  622.4 300.1 all-gather.5
  933.1 96.8 reduce-scatter.7
  1033.4 55.7 reduce-scatter.5
where the time goes:
time: 1100 us
  waiting for transfers between devices  780 us (71%)
  blocking collectives  257 us (23%)
  matrix products  25.9 us (2%)
  between operations  16.3 us (1%)
  local copies, waits for them, and re-layouts  15.4 us (1%)
    unnamed x6, waiting for transfers between devices  325 us
    all_gather x1, waiting for transfers between devices, local(): lax.all_gather(error_local.astype(jnp.bfloat16), 'lat', axis=1, tiled=True)  301 us
    unnamed x1, blocking collectives  140 us
    all_gather x1, waiting for transfers between devices, local(): lax.all_gather(inputs, 'lat', axis=1, tiled=True)  123 us
    psum x1, blocking collectives, local(): squares = lax.psum(jnp.sum(error_local * error_local), ('lat', 'dp'))  118 us
    reduce_scatter x1, waiting for transfers between devices, local(): lax.psum_scatter(lax.dot_general(activations, error_bf, (((0,), (0,)), ((...  31 us
  transfers between devices with their start and end apart: 5, of which 4 were waited for; matrix products, arithmetic and copies ran while one was open for 1% of the time, Pallas kernels for 0%

commit v1 on v0

v1 whole, which is shorter than its diff:
```python
import functools

import jax
import jax.numpy as jnp
from jax import lax
from jax.experimental import pallas as pl
from jax.experimental.pallas import tpu as pltpu
from jax.sharding import PartitionSpec as P

MESH = pl.DeviceIdType.MESH
NX, NY, NZ = 4, 2, 8
NSLOT = NX * NY * NZ
BF16, F32 = jnp.bfloat16, jnp.float32


def place():
    lat = lax.axis_index("lat")
    return lax.div(lat, NY * NZ), lax.rem(lax.div(lat, NZ), NY), lax.rem(lat, NZ)


def slot_id(x, y, z):
    return (lax.rem(x + 2 * NX, NX) * NY + lax.rem(y + 2, NY)) * NZ + lax.rem(z + 2 * NZ, NZ)


def offset(k):
    half = lax.div(k + 1, 2)
    return jnp.where(lax.rem(k, 2) == 1, -half, half)


class Tree:
    def __init__(self, swap):
        self.swap = swap
        self.na, self.nb = (NZ, NX) if swap else (NX, NZ)
        self.x, self.y, self.z = place()

    def sid(self, a, b, j):
        if self.swap:
            return slot_id(self.x + b, self.y + j, self.z + a)
        return slot_id(self.x + a, self.y + j, self.z + b)

    def parity(self, j):
        return lax.rem(self.y + j, 2)

    def column(self, a, j):
        n = self.na
        me = self.z if self.swap else self.x
        return lax.rem(me + a + 2 * n, n) * 2 + self.parity(j)


def wait_for(ref, sem):
    pltpu.make_async_copy(ref, ref, sem).wait()


def gather_tree(buf, send_sem, recv_sem, swap):
    t = Tree(swap)
    na, nb, sid = t.na, t.nb, t.sid

    def send(s, a=0, b=0, j=0):
        pltpu.make_async_remote_copy(
            src_ref=buf.at[s],
            dst_ref=buf.at[s],
            send_sem=send_sem,
            recv_sem=recv_sem.at[s],
            device_id={"lat": sid(a, b, j)},
            device_id_type=MESH,
        ).start()

    def wait(s):
        wait_for(buf.at[s], recv_sem.at[s])

    own, other = sid(0, 0, 0), sid(0, 0, 1)
    send(own, j=1)
    for s in (own, other):
        if s is other:
            wait(other)
        send(s, a=1)
        send(s, a=-1)
        send(s, b=1)
        send(s, b=-1)
    for h in range(1, na // 2 + 1):
        for j in range(2):
            if h < na // 2:
                sm, sp = sid(-h, 0, j), sid(h, 0, j)
                wait(sm)
                if h + 1 < na // 2:
                    send(sm, a=1)
                send(sm, b=1)
                send(sm, b=-1)
                wait(sp)
                if h + 1 < na // 2:
                    send(sp, a=-1)
                send(sp, b=1)
                send(sp, b=-1)
                if h + 1 == na // 2:
                    pl.when(t.parity(j) == 0)(functools.partial(send, sm, a=1))
                    pl.when(t.parity(j) == 1)(functools.partial(send, sp, a=-1))
            else:
                s = sid(h, 0, j)
                wait(s)
                send(s, b=1)
                send(s, b=-1)

    def hop(h, c, carry):
        a, j = offset(lax.div(c, 2)), lax.rem(c, 2)
        if h == nb // 2:
            wait(sid(a, h, j))
            return carry
        sm, sp = sid(a, -h, j), sid(a, h, j)
        wait(sm)
        if h + 1 < nb // 2:
            send(sm, b=1)
        else:
            pl.when(t.parity(j) == 0)(functools.partial(send, sm, b=1))
        wait(sp)
        if h + 1 < nb // 2:
            send(sp, b=-1)
        else:
            pl.when(t.parity(j) == 1)(functools.partial(send, sp, b=-1))
        return carry

    for h in range(1, nb // 2 + 1):
        lax.fori_loop(0, 2 * na, functools.partial(hop, h), 0)
    sent = buf.at[pl.ds(0, NSLOT - 1)]
    wait_for(sent, send_sem)


def scatter_tree(part, r1, r2, a1, a2, y1, send_sem, r1_sem, r2_sem, a1_sem, a2_sem, y1_sem, swap):
    t = Tree(swap)
    na, nb, sid = t.na, t.nb, t.sid

    def send(s, dst, sem, a=0, b=0, j=0):
        pltpu.make_async_remote_copy(
            src_ref=part.at[s],
            dst_ref=dst,
            send_sem=send_sem,
            recv_sem=sem,
            device_id={"lat": sid(a, b, j)},
            device_id_type=MESH,
        ).start()

    def take(s, ref, sem):
        wait_for(ref, sem)
        part[s] += ref[...]

    def col(c):
        k = na - 1 - lax.div(c, 2)
        return offset(k), lax.rem(c, 2)

    far = nb // 2

    def first(c, carry):
        a, j = col(c)
        s = sid(a, far, j)
        pl.when(t.parity(j) == 0)(functools.partial(send, s, r1.at[s], r1_sem.at[s], b=-1))
        pl.when(t.parity(j) == 1)(functools.partial(send, s, r1.at[s], r1_sem.at[s], b=1))
        return carry

    def hop(h, c, carry):
        a, j = col(c)
        sm, sp = sid(a, -h, j), sid(a, h, j)
        if h == far - 1:
            pl.when(t.parity(j) == 0)(functools.partial(take, sm, r1.at[sm], r1_sem.at[sm]))
            pl.when(t.parity(j) == 1)(functools.partial(take, sp, r1.at[sp], r1_sem.at[sp]))
        else:
            take(sm, r1.at[sm], r1_sem.at[sm])
            take(sp, r1.at[sp], r1_sem.at[sp])
        send(sm, r1.at[sm], r1_sem.at[sm], b=-1)
        if h > 1:
            send(sp, r1.at[sp], r1_sem.at[sp], b=1)
        else:
            k = t.column(a, j)
            send(sp, r2.at[k], r2_sem.at[k], b=1)
        return carry

    lax.fori_loop(0, 2 * na, first, 0)
    for h in range(far - 1, 0, -1):
        lax.fori_loop(0, 2 * na, functools.partial(hop, h), 0)

    def own_b(a, j):
        s, k = sid(a, 0, j), t.column(a, j)
        take(s, r1.at[s], r1_sem.at[s])
        take(s, r2.at[k], r2_sem.at[k])
        return s, k

    fara = na // 2
    for j in range(2):
        s, k = own_b(fara, j)
        pl.when(t.parity(j) == 0)(functools.partial(send, s, a1.at[k], a1_sem.at[k], a=-1))
        pl.when(t.parity(j) == 1)(functools.partial(send, s, a1.at[k], a1_sem.at[k], a=1))
    for h in range(fara - 1, 0, -1):
        for j in range(2):
            sm, km = own_b(-h, j)
            sp, kp = own_b(h, j)
            if h == fara - 1:
                pl.when(t.parity(j) == 0)(functools.partial(take, sm, a1.at[km], a1_sem.at[km]))
                pl.when(t.parity(j) == 1)(functools.partial(take, sp, a1.at[kp], a1_sem.at[kp]))
            else:
                take(sm, a1.at[km], a1_sem.at[km])
                take(sp, a1.at[kp], a1_sem.at[kp])
            send(sm, a1.at[km], a1_sem.at[km], a=-1)
            if h > 1:
                send(sp, a1.at[kp], a1_sem.at[kp], a=1)
            else:
                q = t.parity(j)
                send(sp, a2.at[q], a2_sem.at[q], a=1)
    for j in (1, 0):
        s, k = own_b(0, j)
        take(s, a1.at[k], a1_sem.at[k])
        q = t.parity(j)
        take(s, a2.at[q], a2_sem.at[q])
        if j == 1:
            send(s, y1, y1_sem, j=1)
    take(sid(0, 0, 0), y1, y1_sem)
    sent = part.at[pl.ds(0, NSLOT - 1)]
    wait_for(sent, send_sem)


def column_of(row):
    n = row.shape[1]
    eye = lax.broadcasted_iota(jnp.int32, (n, n), 0) == lax.broadcasted_iota(jnp.int32, (n, n), 1)
    return jnp.sum(jnp.where(eye, jnp.broadcast_to(row, (n, n)), 0.0), axis=1, keepdims=True)


def kernel(
    x_ref, bias_ref, enc_hbm, ebias_ref, dec_hbm, other_ref, gate_ref,
    err_ref, mse_ref, gd_ref, ge_ref,
    enc, dec, xt, et, part, r1, r2, a1, a2, y1, act, pos2, cr, ys, yr, sq_z, sq_x, sq_y, sq_t,
    load_sem, ag_send, ag_recv, rs_send, r1_sem, r2_sem, a1_sem, a2_sem, y1_sem,
    ag2_send, ag2_recv, core_send, core_recv, yx_send, yx_recv, sq_send, sq_recv,
):
    x, y, z = place()
    dp = lax.axis_index("dp")
    core, half = lax.rem(dp, 2), lax.div(dp, 2)
    own = slot_id(x, y, z)
    width, rows = x_ref.shape
    lats = dec.shape[0]
    block = lats // gate_ref.shape[0]

    load_e = pltpu.make_async_copy(enc_hbm, enc, load_sem.at[0])
    load_d = pltpu.make_async_copy(dec_hbm, dec, load_sem.at[1])
    load_e.start()
    load_d.start()

    barrier = pltpu.get_barrier_semaphore()
    for k in range(1, NX):
        pl.semaphore_signal(barrier, inc=1, device_id={"lat": slot_id(x + k, y, z)}, device_id_type=MESH)
    for k in range(1, NZ):
        pl.semaphore_signal(barrier, inc=1, device_id={"lat": slot_id(x, y, z + k)}, device_id_type=MESH)
    for k in range(1, 8):
        pl.semaphore_signal(
            barrier,
            inc=1,
            device_id={"lat": slot_id(x, y + k // 4, z), "dp": lax.rem(dp + k, 4)},
            device_id_type=MESH,
        )
    bias_col = column_of(bias_ref[...].astype(F32))
    x_f = x_ref[...].astype(F32)
    xt[own] = (x_f - bias_col).astype(BF16)
    pl.semaphore_wait(barrier, NX - 1 + NZ - 1 + 7)

    for c in range(2):

        @pl.when(core == c)
        def _():
            gather_tree(xt, ag_send, ag_recv, c == 1)

    load_e.wait()
    load_d.wait()

    group = NSLOT // 8
    feats = group * width

    def pre_step(k, acc):
        w = enc[pl.ds(pl.multiple_of(k * feats, feats), feats), :]
        v = xt[pl.ds(k * group, group)].reshape(feats, rows)
        return acc + lax.dot_general(w, v, (((0,), (0,)), ((), ())), preferred_element_type=F32)

    pre = lax.fori_loop(0, 8, pre_step, jnp.zeros((lats, rows), F32))
    positive = jnp.maximum(pre + column_of(ebias_ref[...]), 0.0)
    gate = jnp.concatenate(
        [jnp.broadcast_to(gate_ref[i : i + 1, :].astype(F32), (block, rows)) for i in range(lats // block)], axis=0
    )
    gated = positive * gate
    act[...] = (positive * gated).astype(BF16)
    pos2[...] = 2.0 * gated

    def rec_step(k, carry):
        w = dec[:, pl.ds(pl.multiple_of(k * feats, feats), feats)]
        out = lax.dot_general(w, act[...], (((0,), (0,)), ((), ())), preferred_element_type=F32)
        part[pl.ds(k * group, group)] = out.reshape(group, width, rows)
        return carry

    lax.fori_loop(0, 8, rec_step, 0)

    for c in range(2):

        @pl.when(core == c)
        def _():
            scatter_tree(
                part, r1, r2, a1, a2, y1, rs_send, r1_sem, r2_sem, a1_sem, a2_sem, y1_sem, c == 1
            )

    error = part[own] + other_ref[...] + bias_col - x_f
    err_ref[...] = error
    et[own] = error.astype(BF16)
    sq = error * error
    tile = sum(sq[8 * i : 8 * i + 8] for i in range(width // 8))
    tile = sum(tile[:, 128 * i : 128 * i + 128] for i in range(rows // 128))
    total_rows = rows * 4
    tile = tile * (1.0 / (total_rows * width * NSLOT))

    def spread(dst, mine, level, value, peers):
        dst[mine] = value
        sq_t[level] = value
        for i, dev in enumerate(peers):
            pltpu.make_async_remote_copy(
                src_ref=sq_t.at[level],
                dst_ref=dst.at[mine],
                send_sem=sq_send.at[level],
                recv_sem=sq_recv.at[level],
                device_id=dev,
                device_id_type=MESH,
            ).start()

    def collect(dst, mine, level, n):
        view = dst.at[pl.ds(0, n - 1)]
        wait_for(view, sq_recv.at[level])
        wait_for(view, sq_send.at[level])
        return sum(dst[i] for i in range(n))

    spread(sq_z, z, 0, tile, [{"lat": slot_id(x, y, z + k)} for k in range(1, NZ)])

    for c in range(2):

        @pl.when(core == c)
        def _():
            gather_tree(et, ag2_send, ag2_recv, c == 1)

    tile = collect(sq_z, z, 0, NZ)
    spread(sq_x, x, 1, tile, [{"lat": slot_id(x + k, y, z)} for k in range(1, NX)])

    share = lats // 4
    other_core = lax.rem(core + 1, 2)

    def grad(lhs, rhs, base):
        def step(k, carry):
            v = rhs[pl.ds(k * group, group)].reshape(feats, rows)
            out = lax.dot_general(lhs, v, (((1,), (1,)), ((), ())), preferred_element_type=F32)
            for q in range(4):
                part[base + q * 8 + k] = out[q * share : (q + 1) * share, :]
            return carry

        lax.fori_loop(0, 8, step, 0)

    def core_copy(i, h):
        src = part.at[pl.ds(i * 32 + (h * 2 + other_core) * 8, 8)]
        return pltpu.make_async_remote_copy(
            src_ref=src,
            dst_ref=cr.at[i, h],
            send_sem=core_send.at[i, h],
            recv_sem=core_recv.at[i, h],
            device_id={"dp": half * 2 + other_core},
            device_id_type=MESH,
        )

    def y_copy(i):
        return pltpu.make_async_remote_copy(
            src_ref=ys.at[i],
            dst_ref=yr.at[i],
            send_sem=yx_send.at[i],
            recv_sem=yx_recv.at[i],
            device_id={"dp": (1 - half) * 2 + core},
            device_id_type=MESH,
        )

    def start_core(i):
        core_copy(i, 1 - half).start()
        core_copy(i, half).start()

    def start_y(i):
        h = 1 - half
        core_copy(i, h).wait_recv()
        base = i * 32 + (h * 2 + core) * 8

        def step(k, carry):
            ys[i, k] = (part[base + k] + cr[i, h, k]).astype(BF16)
            return carry

        lax.fori_loop(0, 8, step, 0)
        y_copy(i).start()

    def finish(i, out_ref):
        core_copy(i, half).wait_recv()
        y_copy(i).wait_recv()
        base = i * 32 + (half * 2 + core) * 8
        for k in range(8):
            out_ref[:, k * feats : (k + 1) * feats] = (part[base + k] + cr[i, half, k]) + yr[i, k].astype(F32)
        core_copy(i, 0).wait_send()
        core_copy(i, 1).wait_send()
        y_copy(i).wait_send()

    grad(act[...], et, 0)
    start_core(0)

    def dact_step(k, acc):
        w = dec[:, pl.ds(pl.multiple_of(k * feats, feats), feats)]
        v = et[pl.ds(k * group, group)].reshape(feats, rows)
        return acc + lax.dot_general(w, v, (((1,), (0,)), ((), ())), preferred_element_type=F32)

    dact = lax.fori_loop(0, 8, dact_step, jnp.zeros((lats, rows), F32))
    dpre = (dact * pos2[...]).astype(BF16)
    start_y(0)
    grad(dpre, xt, 32)
    start_core(1)
    tile = collect(sq_x, x, 1, NX)
    mine = y * 4 + dp
    spread(
        sq_y,
        mine,
        2,
        tile,
        [{"lat": slot_id(x, y + k // 4, z), "dp": lax.rem(dp + k, 4)} for k in range(1, 8)],
    )
    start_y(1)
    finish(0, gd_ref)
    tile = collect(sq_y, mine, 2, 8)
    mse_ref[...] = jnp.broadcast_to(jnp.sum(tile, keepdims=True), mse_ref.shape)
    finish(1, ge_ref)


def local(inputs, dec_bias, enc_weight, enc_bias, dec_weight, other_recon, active_blocks):
    rows, width = inputs.shape
    lats, features = dec_weight.shape
    share = lats // 4
    slots = (NSLOT, width, rows)
    vmem = pl.BlockSpec(memory_space=pltpu.VMEM)
    hbm = pl.BlockSpec(memory_space=pl.ANY)
    dma = pltpu.SemaphoreType.DMA
    error, mse, grad_dec, grad_enc = pl.pallas_call(
        kernel,
        name="sae_step",
        out_shape=(
            jax.ShapeDtypeStruct((width, rows), F32),
            jax.ShapeDtypeStruct((8, 128), F32),
            jax.ShapeDtypeStruct((share, features), F32),
            jax.ShapeDtypeStruct((share, features), F32),
        ),
        in_specs=[vmem, vmem, hbm, vmem, hbm, vmem, vmem],
        out_specs=(vmem, vmem, vmem, vmem),
        scratch_shapes=[
            pltpu.VMEM(enc_weight.shape, BF16),
            pltpu.VMEM(dec_weight.shape, BF16),
            pltpu.VMEM(slots, BF16),
            pltpu.VMEM(slots, BF16),
            pltpu.VMEM(slots, F32),
            pltpu.VMEM(slots, F32),
            pltpu.VMEM((2 * NZ, width, rows), F32),
            pltpu.VMEM((2 * NZ, width, rows), F32),
            pltpu.VMEM((2, width, rows), F32),
            pltpu.VMEM((width, rows), F32),
            pltpu.VMEM((lats, rows), BF16),
            pltpu.VMEM((lats, rows), F32),
            pltpu.VMEM((2, 2, 8, share, rows), F32),
            pltpu.VMEM((2, 8, share, rows), BF16),
            pltpu.VMEM((2, 8, share, rows), BF16),
            pltpu.VMEM((NZ, 8, 128), F32),
            pltpu.VMEM((NX, 8, 128), F32),
            pltpu.VMEM((8, 8, 128), F32),
            pltpu.VMEM((3, 8, 128), F32),
            dma((2,)),
            dma,
            dma((NSLOT,)),
            dma,
            dma((NSLOT,)),
            dma((2 * NZ,)),
            dma((2 * NZ,)),
            dma((2,)),
            dma,
            dma,
            dma((NSLOT,)),
            dma((2, 2)),
            dma((2, 2)),
            dma((2,)),
            dma((2,)),
            dma((3,)),
            dma((3,)),
        ],
        compiler_params=pltpu.CompilerParams(
            collective_id=0, has_side_effects=True, vmem_limit_bytes=60 * 2**20
        ),
    )(
        inputs.T,
        dec_bias.reshape(1, -1),
        enc_weight,
        enc_bias.reshape(1, -1),
        dec_weight,
        other_recon.T,
        active_blocks.T,
    )
    return error.T, mse[0, 0], grad_dec, grad_enc.T


def solution(mesh):
    placed = (
        P("dp", "lat"),
        P("lat"),
        P(None, "lat"),
        P("lat"),
        P("lat", None),
        P("dp", "lat"),
        P("dp", "lat"),
    )
    return jax.shard_map(
        local,
        mesh=mesh,
        in_specs=placed,
        out_specs=(P("dp", "lat"), P(), P(("lat", "dp"), None), P(None, ("lat", "dp"))),
        check_vma=False,
    )
```

time: 1100 us -> 183 us (0.17)
  waiting for transfers between devices: 780 us -> 0 us
  blocking collectives: 257 us -> 0 us
  Pallas kernels: 0 us -> 176 us
  matrix products: 25.9 us -> 0 us
  between operations: 16.3 us -> 0.65 us
    all_gather x2 -> x0, waiting for transfers between devices: 424 us -> none  [the longest x1 301 us: local(): lax.all_gather(error_local.astype(jnp.bfloat16), 'lat', axis=1, tiled=True)]
    unnamed x6 -> x0, waiting for transfers between devices: 325 us -> none
    pallas_call x0 -> x1, Pallas kernels: none -> 176 us  [local(): pl.pallas_call(kernel, name='sae_step', out_shape=(jax.ShapeDtypeStruct((...]
    unnamed x1 -> x0, blocking collectives: 140 us -> none
    psum x1 -> x0, blocking collectives: 118 us -> none  [local(): squares = lax.psum(jnp.sum(error_local * error_local), ('lat', 'dp'))]
    reduce_scatter x2 -> x0, waiting for transfers between devices: 31.1 us -> none  [the longest x1 31 us: local(): lax.psum_scatter(lax.dot_general(activations, error_bf, (((0,), (0,)), ((...]
    dot_general x4 -> x0, matrix products: 25.9 us -> none  [the longest x1 10.2 us: local(): lax.dot_general(centered, dpre, (((0,), (0,)), ((), ())), preferred_eleme...]
  transfers between devices with their start and end apart: 5 -> 0, of which waited for: 4 -> 0; matrix products, arithmetic and copies ran while one was open for 1% -> 0% of each run, Pallas kernels for 0% -> 0%
where the time goes in v1:
time: 183 us; the launch traced here: 182 us
  Pallas kernels  176 us (96%)
  local copies, waits for them, and re-layouts  6.09 us (3%)
    pallas_call x1, Pallas kernels, local(): pl.pallas_call(kernel, name='sae_step', out_shape=(jax.ShapeDtypeStruct((...  176 us
    unnamed x5, local copies, waits for them, and re-layouts  4.81 us

profile of v1, /device:TPU:1, one launch (start us, length us, event | category | flops | bytes accessed | tf_op | source)
XLA Modules:
  0.0 182.5 jit_solution(11766342863996514726)
XLA Ops:
  0.6 175.7 %sae_step.1 = (f32[64,512]{1,0:T(8,128)}, f32[8,128]{1,0:T(8,128)}, f32[64,4096]{1,0:T(8,128)}, f32[64,4096]{1,0:T(8,128)}) custom-call(bf16[64,512]{1,0:T(8,128)(2,1)} %bitcast.11, bf16[1,64]{1,0:T(2,128)(2,1)} %bitcast.14, bf16[4096,256]{1,0:T(8,128)(2,1)} %enc_hbm.1, f32[1,256]{1,0:T(1,128)} %bitcast.13, bf16[256,4096]{1,0:T(8,128)(2,1)} %dec_hbm.1, ...), custom_call_target="tpu_custom_call" | custom-call | tf_op jit(solution)/shard_map/sae_step/pallas_call | solution.py:439
  176.4 0.0 copy-start
  176.4 1.3 slice.3
  177.7 1.6 copy.14
  179.2 2.3 %copy.15 = f32[64,4096]{1,0:T(8,128)} copy(f32[64,4096]{1,0:T(8,128)} %get-tuple-element.18) | data formatting | bytes 2097152
  181.5 0.0 copy-done
  181.5 1.0 copy.16
Async XLA Ops:
  176.4 5.1 %copy-start = (f32[64,4096]{1,0:T(8,128)S(1)}, f32[64,4096]{1,0:T(8,128)}, u32[]{:S(2)}) copy-start(f32[64,4096]{1,0:T(8,128)} %get-tuple-element.11) | copy-start | bytes 3145732

commit v2 on v1

--- a/solution.py
+++ b/solution.py
@@ -124,23 +124,51 @@
     wait_for(sent, send_sem)
 
 
-def scatter_tree(part, r1, r2, a1, a2, y1, send_sem, r1_sem, r2_sem, a1_sem, a2_sem, y1_sem, swap):
+def over_tiles(v):
+    w, r = v.shape
+    return [[v[8 * i : 8 * i + 8, 128 * k : 128 * k + 128] for k in range(r // 128)] for i in range(w // 8)]
+
+
+def tiled(tile, shape):
+    row = jnp.concatenate([tile] * (shape[1] // 128), axis=1)
+    return jnp.concatenate([row] * (shape[0] // 8), axis=0)
+
+
+LEVELS = 32000.0
+
+
+def encode(v):
+    top = functools.reduce(
+        jnp.maximum, [functools.reduce(jnp.maximum, [jnp.abs(t) for t in line]) for line in over_tiles(v)]
+    )
+    top = jnp.maximum(top, 1e-30)
+    return jnp.round(v * tiled(LEVELS / top, v.shape)).astype(jnp.int16), top * (1.0 / LEVELS)
+
+
+def decode(q, scale):
+    return q.astype(F32) * tiled(scale, q.shape)
+
+
+def scatter_tree(part, out, r1, r2, a1, a2, y1, send_sem, r1_sem, r2_sem, a1_sem, a2_sem, y1_sem, swap):
     t = Tree(swap)
     na, nb, sid = t.na, t.nb, t.sid
 
-    def send(s, dst, sem, a=0, b=0, j=0):
-        pltpu.make_async_remote_copy(
-            src_ref=part.at[s],
-            dst_ref=dst,
-            send_sem=send_sem,
-            recv_sem=sem,
-            device_id={"lat": sid(a, b, j)},
-            device_id_type=MESH,
-        ).start()
-
-    def take(s, ref, sem):
-        wait_for(ref, sem)
-        part[s] += ref[...]
+    def send(s, dst, k, sem, a=0, b=0, j=0):
+        out[0][s], out[1][s] = encode(part[s])
+        for i in range(2):
+            pltpu.make_async_remote_copy(
+                src_ref=out[i].at[s],
+                dst_ref=dst[i].at[k],
+                send_sem=send_sem.at[i],
+                recv_sem=sem.at[i, k],
+                device_id={"lat": sid(a, b, j)},
+                device_id_type=MESH,
+            ).start()
+
+    def take(s, ref, k, sem):
+        for i in range(2):
+            wait_for(ref[i].at[k], sem.at[i, k])
+        part[s] += decode(ref[0][k], ref[1][k])
 
     def col(c):
         k = na - 1 - lax.div(c, 2)
@@ -151,25 +179,25 @@
     def first(c, carry):
         a, j = col(c)
         s = sid(a, far, j)
-        pl.when(t.parity(j) == 0)(functools.partial(send, s, r1.at[s], r1_sem.at[s], b=-1))
-        pl.when(t.parity(j) == 1)(functools.partial(send, s, r1.at[s], r1_sem.at[s], b=1))
+        pl.when(t.parity(j) == 0)(functools.partial(send, s, r1, s, r1_sem, b=-1))
+        pl.when(t.parity(j) == 1)(functools.partial(send, s, r1, s, r1_sem, b=1))
         return carry
 
     def hop(h, c, carry):
         a, j = col(c)
         sm, sp = sid(a, -h, j), sid(a, h, j)
         if h == far - 1:
-            pl.when(t.parity(j) == 0)(functools.partial(take, sm, r1.at[sm], r1_sem.at[sm]))
-            pl.when(t.parity(j) == 1)(functools.partial(take, sp, r1.at[sp], r1_sem.at[sp]))
+            pl.when(t.parity(j) == 0)(functools.partial(take, sm, r1, sm, r1_sem))
+            pl.when(t.parity(j) == 1)(functools.partial(take, sp, r1, sp, r1_sem))
         else:
-            take(sm, r1.at[sm], r1_sem.at[sm])
-            take(sp, r1.at[sp], r1_sem.at[sp])
-        send(sm, r1.at[sm], r1_sem.at[sm], b=-1)
+            take(sm, r1, sm, r1_sem)
+        send(sm, r1, sm, r1_sem, b=-1)
+        if h < far - 1:
+            take(sp, r1, sp, r1_sem)
         if h > 1:
-            send(sp, r1.at[sp], r1_sem.at[sp], b=1)
+            send(sp, r1, sp, r1_sem, b=1)
         else:
-            k = t.column(a, j)
-            send(sp, r2.at[k], r2_sem.at[k], b=1)
+            send(sp, r2, t.column(a, j), r2_sem, b=1)
         return carry
 
     lax.fori_loop(0, 2 * na, first, 0)
@@ -178,41 +206,39 @@
 
     def own_b(a, j):
         s, k = sid(a, 0, j), t.column(a, j)
-        take(s, r1.at[s], r1_sem.at[s])
-        take(s, r2.at[k], r2_sem.at[k])
+        take(s, r1, s, r1_sem)
+        take(s, r2, k, r2_sem)
         return s, k
 
     fara = na // 2
     for j in range(2):
         s, k = own_b(fara, j)
-        pl.when(t.parity(j) == 0)(functools.partial(send, s, a1.at[k], a1_sem.at[k], a=-1))
-        pl.when(t.parity(j) == 1)(functools.partial(send, s, a1.at[k], a1_sem.at[k], a=1))
+        pl.when(t.parity(j) == 0)(functools.partial(send, s, a1, k, a1_sem, a=-1))
+        pl.when(t.parity(j) == 1)(functools.partial(send, s, a1, k, a1_sem, a=1))
     for h in range(fara - 1, 0, -1):
         for j in range(2):
             sm, km = own_b(-h, j)
             sp, kp = own_b(h, j)
             if h == fara - 1:
-                pl.when(t.parity(j) == 0)(functools.partial(take, sm, a1.at[km], a1_sem.at[km]))
-                pl.when(t.parity(j) == 1)(functools.partial(take, sp, a1.at[kp], a1_sem.at[kp]))
+                pl.when(t.parity(j) == 0)(functools.partial(take, sm, a1, km, a1_sem))
+                pl.when(t.parity(j) == 1)(functools.partial(take, sp, a1, kp, a1_sem))
             else:
-                take(sm, a1.at[km], a1_sem.at[km])
-                take(sp, a1.at[kp], a1_sem.at[kp])
-            send(sm, a1.at[km], a1_sem.at[km], a=-1)
+                take(sm, a1, km, a1_sem)
+                take(sp, a1, kp, a1_sem)
+            send(sm, a1, km, a1_sem, a=-1)
             if h > 1:
-                send(sp, a1.at[kp], a1_sem.at[kp], a=1)
+                send(sp, a1, kp, a1_sem, a=1)
             else:
-                q = t.parity(j)
-                send(sp, a2.at[q], a2_sem.at[q], a=1)
+                send(sp, a2, t.parity(j), a2_sem, a=1)
     for j in (1, 0):
         s, k = own_b(0, j)
-        take(s, a1.at[k], a1_sem.at[k])
-        q = t.parity(j)
-        take(s, a2.at[q], a2_sem.at[q])
+        take(s, a1, k, a1_sem)
+        take(s, a2, t.parity(j), a2_sem)
         if j == 1:
-            send(s, y1, y1_sem, j=1)
-    take(sid(0, 0, 0), y1, y1_sem)
-    sent = part.at[pl.ds(0, NSLOT - 1)]
-    wait_for(sent, send_sem)
+            send(s, y1, 0, y1_sem, j=1)
+    take(sid(0, 0, 0), y1, 0, y1_sem)
+    for i in range(2):
+        wait_for(out[i].at[pl.ds(0, NSLOT - 1)], send_sem.at[i])
 
 
 def column_of(row):
@@ -224,7 +250,7 @@
 def kernel(
     x_ref, bias_ref, enc_hbm, ebias_ref, dec_hbm, other_ref, gate_ref,
     err_ref, mse_ref, gd_ref, ge_ref,
-    enc, dec, xt, et, part, r1, r2, a1, a2, y1, act, pos2, cr, ys, yr, sq_z, sq_x, sq_y, sq_t,
+    enc, dec, xt, et, part, out_q, out_s, r1_q, r1_s, r2_q, r2_s, a1_q, a1_s, a2_q, a2_s, y1_q, y1_s, act, pos2, cr, ys, yr, sq_z, sq_x, sq_y, sq_t,
     load_sem, ag_send, ag_recv, rs_send, r1_sem, r2_sem, a1_sem, a2_sem, y1_sem,
     ag2_send, ag2_recv, core_send, core_recv, yx_send, yx_recv, sq_send, sq_recv,
 ):
@@ -297,7 +323,8 @@
         @pl.when(core == c)
         def _():
             scatter_tree(
-                part, r1, r2, a1, a2, y1, rs_send, r1_sem, r2_sem, a1_sem, a2_sem, y1_sem, c == 1
+                part, (out_q, out_s), (r1_q, r1_s), (r2_q, r2_s), (a1_q, a1_s), (a2_q, a2_s), (y1_q, y1_s),
+                rs_send, r1_sem, r2_sem, a1_sem, a2_sem, y1_sem, c == 1,
             )
 
     error = part[own] + other_ref[...] + bias_col - x_f
@@ -436,6 +463,10 @@
     vmem = pl.BlockSpec(memory_space=pltpu.VMEM)
     hbm = pl.BlockSpec(memory_space=pl.ANY)
     dma = pltpu.SemaphoreType.DMA
+
+    def coded(n):
+        return pltpu.VMEM((n, width, rows), jnp.int16), pltpu.VMEM((n, 8, 128), F32)
+
     error, mse, grad_dec, grad_enc = pl.pallas_call(
         kernel,
         name="sae_step",
@@ -453,11 +484,12 @@
             pltpu.VMEM(slots, BF16),
             pltpu.VMEM(slots, BF16),
             pltpu.VMEM(slots, F32),
-            pltpu.VMEM(slots, F32),
-            pltpu.VMEM((2 * NZ, width, rows), F32),
-            pltpu.VMEM((2 * NZ, width, rows), F32),
-            pltpu.VMEM((2, width, rows), F32),
-            pltpu.VMEM((width, rows), F32),
+            *coded(NSLOT),
+            *coded(NSLOT),
+            *coded(2 * NZ),
+            *coded(2 * NZ),
+            *coded(2),
+            *coded(1),
             pltpu.VMEM((lats, rows), BF16),
             pltpu.VMEM((lats, rows), F32),
             pltpu.VMEM((2, 2, 8, share, rows), F32),
@@ -470,12 +502,12 @@
             dma((2,)),
             dma,
             dma((NSLOT,)),
-            dma,
-            dma((NSLOT,)),
-            dma((2 * NZ,)),
-            dma((2 * NZ,)),
             dma((2,)),
-            dma,
+            dma((2, NSLOT)),
+            dma((2, 2 * NZ)),
+            dma((2, 2 * NZ)),
+            dma((2, 2)),
+            dma((2, 1)),
             dma,
             dma((NSLOT,)),
             dma((2, 2)),

time: 183 us -> 157 us (0.86)
  Pallas kernels: 176 us -> 150 us
    pallas_call x1, Pallas kernels: 176 us -> 150 us  [local(): pl.pallas_call(kernel, name='sae_step', out_shape=(jax.ShapeDtypeStruct((...]
where the time goes in v2:
time: 157 us
  Pallas kernels  150 us (96%)
  local copies, waits for them, and re-layouts  6.09 us (4%)
    pallas_call x1, Pallas kernels, local(): pl.pallas_call(kernel, name='sae_step', out_shape=(jax.ShapeDtypeStruct((...  150 us
    unnamed x5, local copies, waits for them, and re-layouts  4.81 us

profile of v2, /device:TPU:1, one launch (start us, length us, event | category | flops | bytes accessed | tf_op | source)
XLA Modules:
  0.0 156.8 jit_solution(15192838367437048111)
XLA Ops:
  0.6 150.0 %sae_step.1 = (f32[64,512]{1,0:T(8,128)}, f32[8,128]{1,0:T(8,128)}, f32[64,4096]{1,0:T(8,128)}, f32[64,4096]{1,0:T(8,128)}) custom-call(bf16[64,512]{1,0:T(8,128)(2,1)} %bitcast.11, bf16[1,64]{1,0:T(2,128)(2,1)} %bitcast.14, bf16[4096,256]{1,0:T(8,128)(2,1)} %enc_hbm.1, f32[1,256]{1,0:T(1,128)} %bitcast.13, bf16[256,4096]{1,0:T(8,128)(2,1)} %dec_hbm.1, ...), custom_call_target="tpu_custom_call" | custom-call | tf_op jit(solution)/shard_map/sae_step/pallas_call | solution.py:470
  150.7 0.0 copy-start
  150.7 1.3 slice.3
  152.0 1.6 copy.14
  153.5 2.3 %copy.15 = f32[64,4096]{1,0:T(8,128)} copy(f32[64,4096]{1,0:T(8,128)} %get-tuple-element.18) | data formatting | bytes 2097152
  155.8 0.0 copy-done
  155.8 1.0 copy.16
Async XLA Ops:
  150.7 5.1 %copy-start = (f32[64,4096]{1,0:T(8,128)S(1)}, f32[64,4096]{1,0:T(8,128)}, u32[]{:S(2)}) copy-start(f32[64,4096]{1,0:T(8,128)} %get-tuple-element.11) | copy-start | bytes 3145732

commit v3 on v0

v3 whole, which is shorter than its diff:
```python
import functools

import jax
import jax.numpy as jnp
from jax import lax
from jax.experimental import pallas as pl
from jax.experimental.pallas import tpu as pltpu
from jax.sharding import PartitionSpec as P

MESH = pl.DeviceIdType.MESH
NX, NY, NZ = 4, 2, 8
NSLOT = NX * NY * NZ
GROUP = 8
BF16, F32 = jnp.bfloat16, jnp.float32


def place():
    lat = lax.axis_index("lat")
    return lax.div(lat, NY * NZ), lax.rem(lax.div(lat, NZ), NY), lax.rem(lat, NZ)


def slot_id(x, y, z):
    return (lax.rem(x + 2 * NX, NX) * NY + lax.rem(y + 2, NY)) * NZ + lax.rem(z + 2 * NZ, NZ)


def offset(k):
    half = lax.div(k + 1, 2)
    return jnp.where(lax.rem(k, 2) == 1, -half, half)


class Tree:
    def __init__(self, t):
        self.t = t
        self.na, self.nb = (NZ, NX) if t else (NX, NZ)
        self.x, self.y, self.z = place()

    def sid(self, a, b, j):
        if self.t:
            return slot_id(self.x + b, self.y + j, self.z + a)
        return slot_id(self.x + a, self.y + j, self.z + b)

    def parity(self, j):
        return lax.rem(self.y + j, 2)

    def row(self, a):
        n = self.na
        return lax.rem((self.z if self.t else self.x) + a + 2 * n, n)

    def column(self, a, j):
        return self.row(a) * 2 + self.parity(j)

    def chunks(self, b):
        if self.t:
            base = lax.rem(self.x + b + 2 * NX, NX) * NY
            return [(base + i, [(base + i) * GROUP + k for k in range(GROUP)]) for i in range(NY)]
        base = lax.rem(self.z + b + 2 * NZ, NZ)
        return [(base, [base + NZ * k for k in range(GROUP)])]


def wait_for(ref, sem):
    pltpu.make_async_copy(ref, ref, sem).wait()


def each(n, *bodies):
    def step(c, carry):
        for body in bodies:
            body(c)
        return carry

    lax.fori_loop(0, n, step, 0)


class Gather:
    def __init__(self, t, buf, send_sem, recv_sem):
        self.tree = Tree(t)
        self.buf, self.send_sem, self.recv_sem = buf.at[t], send_sem.at[t], recv_sem.at[t]

    def send(self, s, a=0, b=0, j=0):
        pltpu.make_async_remote_copy(
            src_ref=self.buf.at[s],
            dst_ref=self.buf.at[s],
            send_sem=self.send_sem,
            recv_sem=self.recv_sem.at[s],
            device_id={"lat": self.tree.sid(a, b, j)},
            device_id_type=MESH,
        ).start()

    def wait(self, s):
        wait_for(self.buf.at[s], self.recv_sem.at[s])

    def onward(self, s):
        self.send(s, b=1)
        self.send(s, b=-1)

    def own(self):
        s = self.tree.sid(0, 0, 0)
        self.send(s, a=1)
        self.send(s, a=-1)
        self.send(s, j=1)
        self.onward(s)

    def from_y(self, a):
        s = self.tree.sid(a, 0, 1)
        self.wait(s)
        self.onward(s)

    def ring_a(self, h):
        t = self.tree
        far = t.na // 2
        for d in (-1, 1) if h < far else (1,):
            s = t.sid(d * h, 0, 0)
            self.wait(s)
            if h + 1 < far:
                self.send(s, a=-d)
            elif h < far:
                pl.when(t.y == (d + 1) // 2)(functools.partial(self.send, s, a=-d))
            self.send(s, j=1)
            self.onward(s)
        self.from_y(1 - h)
        if h > 1:
            self.from_y(h - 1)
        if h == far:
            self.from_y(h)

    def ring_b(self, h, c):
        t = self.tree
        far = t.nb // 2
        a, j = offset(lax.div(c, 2)), lax.rem(c, 2)
        if h == far:
            self.wait(t.sid(a, h, j))
            return
        for d in (-1, 1):
            s = t.sid(a, d * h, j)
            self.wait(s)
            if h + 1 < far:
                self.send(s, b=-d)
            else:
                pl.when(t.parity(j) == (d + 1) // 2)(functools.partial(self.send, s, b=-d))

    def end(self):
        wait_for(self.buf.at[pl.ds(0, NSLOT - 1)], self.send_sem)


def gather(buf, send_sem, recv_sem, eat, idle):
    p, q = (Gather(t, buf, send_sem, recv_sem) for t in range(2))

    def eat_all(g, *offsets):
        for b in offsets:
            for index, slots in g.tree.chunks(b):
                eat(g.tree.t, index, slots)

    p.own()
    q.own()
    p.ring_a(1)
    q.ring_a(1)
    p.ring_a(2)
    q.ring_a(2)
    q.ring_a(3)
    each(8, lambda c: p.ring_b(1, c))
    q.ring_a(4)
    idle(0)
    eat_all(p, 0)
    each(8, lambda c: p.ring_b(2, c), lambda c: q.ring_b(1, c))
    eat_all(p, -1, 1)
    eat_all(q, 0)
    idle(1)
    each(8, lambda c: p.ring_b(3, c), lambda c: q.ring_b(1, c + 8))
    eat_all(p, -2, 2)
    eat_all(q, -1, 1)
    idle(2)
    each(8, lambda c: p.ring_b(4, c), lambda c: q.ring_b(2, c))
    each(8, lambda c: q.ring_b(2, c + 8))
    eat_all(p, -3, 3, 4)
    eat_all(q, 2)
    idle(3)
    p.end()
    q.end()


def tiled(row, shape):
    return jnp.broadcast_to(jnp.concatenate([row] * (shape[1] // 128), axis=1), shape)


LEVELS = 32000.0


def encode(v):
    size = jnp.abs(v)
    top = functools.reduce(jnp.maximum, [size[:, i : i + 128] for i in range(0, v.shape[1], 128)])
    top = jnp.maximum(jnp.max(top, axis=0, keepdims=True), 1e-30)
    return jnp.round(v * tiled(LEVELS / top, v.shape)).astype(jnp.int16), top * (1.0 / LEVELS)


def decode(q, scale):
    return q.astype(F32) * tiled(scale, q.shape)


class Scatter:
    def __init__(self, t, part, out, r1, r2, y1, a1, a2, send_sem, r1_sem, r2_sem, y1_sem, a1_sem, a2_sem):
        self.tree = Tree(t)
        self.part = part.at[t]
        self.out, self.send_sem = [o.at[t] for o in out], [send_sem.at[t, i] for i in range(2)]
        bufs = {"r1": (r1, r1_sem), "r2": (r2, r2_sem), "y1": (y1, y1_sem), "a1": (a1, a1_sem), "a2": (a2, a2_sem)}
        self.bufs = {
            name: ([r.at[t] for r in refs], [sem.at[t, i] for i in range(2)]) for name, (refs, sem) in bufs.items()
        }

    def send(self, s, name, k, a=0, b=0, j=0):
        self.out[0][s], self.out[1][s] = encode(self.part[s])
        refs, sems = self.bufs[name]
        for i in range(2):
            pltpu.make_async_remote_copy(
                src_ref=self.out[i].at[s],
                dst_ref=refs[i].at[k],
                send_sem=self.send_sem[i],
                recv_sem=sems[i].at[k],
                device_id={"lat": self.tree.sid(a, b, j)},
                device_id_type=MESH,
            ).start()

    def take(self, s, name, k):
        refs, sems = self.bufs[name]
        for i in range(2):
            wait_for(refs[i].at[k], sems[i].at[k])
        self.part[s] += decode(refs[0][k], refs[1][k])

    def col(self, c):
        return offset(self.tree.na - 1 - lax.div(c, 2)), 1 - lax.rem(c, 2)

    def first(self, c):
        t = self.tree
        a, j = self.col(c)
        s = t.sid(a, t.nb // 2, j)
        for d in (-1, 1):
            pl.when(t.parity(j) == (d + 1) // 2)(functools.partial(self.send, s, "r1", s, b=d))

    def hop(self, h, c):
        t = self.tree
        a, j = self.col(c)
        for d in (-1, 1):
            s = t.sid(a, d * h, j)
            if h == t.nb // 2 - 1:
                pl.when(t.parity(j) == (d + 1) // 2)(functools.partial(self.take, s, "r1", s))
            else:
                self.take(s, "r1", s)
            if h == 1 and d == 1:
                self.send(s, "r2", t.column(a, j), b=d)
            else:
                self.send(s, "r1", s, b=d)

    def own_b(self, a, j):
        s = self.tree.sid(a, 0, j)
        self.take(s, "r1", s)
        self.take(s, "r2", self.tree.column(a, j))
        return s

    def to_y(self, *offsets):
        for a in offsets:
            self.send(self.own_b(a, 1), "y1", self.tree.row(a), j=1)

    def with_y(self, a):
        s, k = self.own_b(a, 0), self.tree.row(a)
        self.take(s, "y1", k)
        return s, k

    def ring_a(self, h):
        t = self.tree
        far = t.na // 2
        if h == far:
            s, k = self.with_y(h)
            for d in (-1, 1):
                pl.when(t.y == (d + 1) // 2)(functools.partial(self.send, s, "a1", k, a=d))
            return
        if h == 0:
            s, k = self.with_y(0)
            self.take(s, "a1", k)
            self.take(s, "a2", 0)
            return
        for d in (-1, 1):
            s, k = self.with_y(d * h)
            if h == far - 1:
                pl.when(t.y == (d + 1) // 2)(functools.partial(self.take, s, "a1", k))
            else:
                self.take(s, "a1", k)
            if h == 1 and d == 1:
                self.send(s, "a2", 0, a=d)
            else:
                self.send(s, "a1", k, a=d)

    def end(self):
        for i in range(2):
            wait_for(self.out[i].at[pl.ds(0, NSLOT - 1)], self.send_sem[i])


def scatter(make, *refs):
    p, q = (Scatter(t, *refs) for t in range(2))

    def make_all(g, *offsets):
        for b in offsets:
            for _, slots in g.tree.chunks(b):
                make(g.tree.t, slots)

    make_all(p, 4)
    make_all(q, 2)
    each(8, p.first, q.first)
    make_all(p, -3, 3)
    each(8, lambda c: p.hop(3, c), lambda c: q.first(c + 8))
    make_all(q, -1, 1)
    make_all(p, -2, 2)
    each(8, lambda c: p.hop(2, c), lambda c: q.hop(1, c))
    make_all(p, -1, 1, 0)
    make_all(q, 0)
    each(8, lambda c: p.hop(1, c), lambda c: q.hop(1, c + 8))
    q.to_y(4, -3, 3)
    p.to_y(2, -1, 1)
    q.ring_a(4)
    q.to_y(-2, 2)
    p.ring_a(2)
    q.ring_a(3)
    q.to_y(-1, 1)
    p.to_y(0)
    q.ring_a(2)
    p.ring_a(1)
    q.to_y(0)
    q.ring_a(1)
    p.ring_a(0)
    q.ring_a(0)
    p.end()
    q.end()


def column_of(row):
    n = row.shape[1]
    eye = lax.broadcasted_iota(jnp.int32, (n, n), 0) == lax.broadcasted_iota(jnp.int32, (n, n), 1)
    return jnp.sum(jnp.where(eye, jnp.broadcast_to(row, (n, n)), 0.0), axis=1, keepdims=True)


def kernel(
    x_ref, bias_ref, enc_hbm, ebias_ref, dec_hbm, other_ref, gate_ref,
    err_ref, mse_ref, own_out, far_out,
    enc, dec, dec_t, xt, et, part, out_q, out_s, r1_q, r1_s, r2_q, r2_s, y1_q, y1_s, a1_q, a1_s, a2_q, a2_s,
    pre, act, pos2, dact, grads, cr, ys, kept, sq_z, sq_x, sq_y, sq_t,
    load_sem, ag_send, ag_recv, rs_send, r1_sem, r2_sem, y1_sem, a1_sem, a2_sem,
    ag2_send, ag2_recv, core_send, core_recv, yx_send, yx_recv, keep_sem, sq_send, sq_recv,
):
    x, y, z = place()
    dp = lax.axis_index("dp")
    core, half = lax.rem(dp, 2), lax.div(dp, 2)
    own = slot_id(x, y, z)
    width, rows = x_ref.shape
    tall = width // 2
    lats = dec.shape[0]
    block = lats // gate_ref.shape[0]

    loads = [pltpu.make_async_copy(enc_hbm.at[:, t], enc.at[t], load_sem.at[t]) for t in range(2)]
    loads.append(pltpu.make_async_copy(dec_hbm, dec, load_sem.at[2]))
    for load in loads:
        load.start()

    barrier = pltpu.get_barrier_semaphore()
    for k in range(1, NX):
        pl.semaphore_signal(barrier, inc=1, device_id={"lat": slot_id(x + k, y, z)}, device_id_type=MESH)
    for k in range(1, NZ):
        pl.semaphore_signal(barrier, inc=1, device_id={"lat": slot_id(x, y, z + k)}, device_id_type=MESH)
    for k in range(1, 8):
        pl.semaphore_signal(
            barrier,
            inc=1,
            device_id={"lat": slot_id(x, y + k // 4, z), "dp": lax.rem(dp + k, 4)},
            device_id_type=MESH,
        )
    bias_col = column_of(bias_ref[...].astype(F32))
    x_f = x_ref[...].astype(F32)
    centered = (x_f - bias_col).astype(BF16)
    for t in range(2):
        xt[t, own] = centered[t * tall : (t + 1) * tall]
    pl.semaphore_wait(barrier, NX - 1 + NZ - 1 + 7)

    def stack(ref, t, slots):
        return jnp.concatenate([ref[t, s] for s in slots], axis=0)

    def encode_chunk(t, index, slots):
        pre[...] += lax.dot_general(
            stack(enc, t, slots), stack(xt, t, slots), (((0,), (0,)), ((), ())), preferred_element_type=F32
        )

    def turn(k):
        if k == 0:
            for load in loads:
                load.wait()
            pre[...] = jnp.broadcast_to(column_of(ebias_ref[...]), pre.shape)
        if k == 1:
            for i in range(NSLOT // 2):
                both = dec[:, 2 * i * width : 2 * (i + 1) * width].T
                for n in range(4):
                    dec_t[n % 2, 2 * i + n // 2] = both[n * tall : (n + 1) * tall]

    gather(xt, ag_send, ag_recv, encode_chunk, turn)

    positive = jnp.maximum(pre[...], 0.0)
    gate = jnp.concatenate(
        [jnp.broadcast_to(gate_ref[i : i + 1, :].astype(F32), (block, rows)) for i in range(lats // block)], axis=0
    )
    gated = positive * gate
    act[...] = (positive * gated).astype(BF16)
    pos2[...] = 2.0 * gated

    def decode_chunk(t, slots):
        out = jnp.dot(stack(dec_t, t, slots), act[...], preferred_element_type=F32)
        for i, s in enumerate(slots):
            part[t, s] = out[i * tall : (i + 1) * tall]

    scatter(
        decode_chunk, part, (out_q, out_s), (r1_q, r1_s), (r2_q, r2_s), (y1_q, y1_s), (a1_q, a1_s), (a2_q, a2_s),
        rs_send, r1_sem, r2_sem, y1_sem, a1_sem, a2_sem,
    )

    total = jnp.concatenate([part[t, own] for t in range(2)], axis=0)
    error = total + other_ref[...] + bias_col - x_f
    err_ref[...] = error
    for t in range(2):
        et[t, own] = error[t * tall : (t + 1) * tall].astype(BF16)
    sq = error * error
    tile = sum(sq[8 * i : 8 * i + 8] for i in range(width // 8))
    tile = sum(tile[:, 128 * i : 128 * i + 128] for i in range(rows // 128))
    tile = tile * (1.0 / (rows * 4 * width * NSLOT))

    def spread(dst, mine, level, value, peers):
        dst[mine] = value
        sq_t[level] = value
        for dev in peers:
            pltpu.make_async_remote_copy(
                src_ref=sq_t.at[level],
                dst_ref=dst.at[mine],
                send_sem=sq_send.at[level],
                recv_sem=sq_recv.at[level],
                device_id=dev,
                device_id_type=MESH,
            ).start()

    def collect(dst, level, n):
        view = dst.at[pl.ds(0, n - 1)]
        wait_for(view, sq_recv.at[level])
        wait_for(view, sq_send.at[level])
        return sum(dst[i] for i in range(n))

    share = lats // 4
    other_core = lax.rem(core + 1, 2)

    def core_copy(i, t, index):
        return pltpu.make_async_remote_copy(
            src_ref=grads.at[i, t, index, other_core],
            dst_ref=cr.at[i, t, index],
            send_sem=core_send.at[i, t, index],
            recv_sem=core_recv.at[i, t, index],
            device_id={"dp": half * 2 + other_core},
            device_id_type=MESH,
        )

    def y_copy(i, t, index):
        return pltpu.make_async_remote_copy(
            src_ref=ys.at[i, t, index],
            dst_ref=far_out.at[i, t, index],
            send_sem=yx_send.at[i, t, index],
            recv_sem=yx_recv.at[i, t, index],
            device_id={"dp": (1 - half) * 2 + core},
            device_id_type=MESH,
        )

    def partial(i, t, index, slots, lhs, ref):
        out = lax.dot_general(lhs, stack(ref, t, slots), (((1,), (1,)), ((), ())), preferred_element_type=F32)
        for h in range(2):
            for c in range(2):
                n = h * 2 + c
                grads[i, t, index, c, h] = out[n * share : (n + 1) * share]
        core_copy(i, t, index).start()

    def exchange(i, t, index):
        core_copy(i, t, index).wait_recv()
        ys[i, t, index] = (grads[i, t, index, core, 1 - half] + cr[i, t, index, 1 - half]).astype(BF16)
        y_copy(i, t, index).start()
        kept[i, t, index] = grads[i, t, index, core, half] + cr[i, t, index, half]

    ready, batch = [], []

    def error_chunk(t, index, slots):
        partial(0, t, index, slots, act[...], et)
        dact[...] += lax.dot_general(
            stack(dec_t, t, slots), stack(et, t, slots), (((0,), (0,)), ((), ())), preferred_element_type=F32
        )
        batch.append((t, index))

    def between(k):
        for t, index in ready:
            exchange(0, t, index)
        ready[:] = batch
        batch.clear()

    spread(sq_z, z, 0, tile, [{"lat": slot_id(x, y, z + k)} for k in range(1, NZ)])
    dact[...] = jnp.zeros(dact.shape, F32)
    gather(et, ag2_send, ag2_recv, error_chunk, between)
    tile = collect(sq_z, 0, NZ)
    spread(sq_x, x, 1, tile, [{"lat": slot_id(x + k, y, z)} for k in range(1, NX)])
    dpre = (dact[...] * pos2[...]).astype(BF16)

    trees = [Tree(t) for t in range(2)]
    for t in range(2):

        def step(index, carry):
            slots = [index * GROUP + k if t else index + NZ * k for k in range(GROUP)]
            partial(1, t, index, slots, dpre, xt)
            return carry

        lax.fori_loop(0, 8, step, 0)
        if t == 0:
            between(4)
    for t in range(2):

        def step(index, carry):
            exchange(1, t, index)
            return carry

        lax.fori_loop(0, 8, step, 0)

    keeps = [pltpu.make_async_copy(kept.at[i], own_out.at[i], keep_sem.at[i]) for i in range(2)]
    for keep in keeps:
        keep.start()
    tile = collect(sq_x, 1, NX)
    peers = [{"lat": slot_id(x, y + k // 4, z), "dp": lax.rem(dp + k, 4)} for k in range(1, 8)]
    spread(sq_y, y * 4 + dp, 2, tile, peers)
    tile = collect(sq_y, 2, 8)
    mse_ref[...] = jnp.broadcast_to(jnp.sum(tile, keepdims=True), mse_ref.shape)
    for i in range(2):
        for t in range(2):

            def step(index, carry):
                core_copy(i, t, index).wait_send()
                y_copy(i, t, index).wait()
                return carry

            lax.fori_loop(0, 8, step, 0)
    for keep in keeps:
        keep.wait()


def finish(own_ref, far_ref, err_ref, mse_ref, gd_ref, ge_ref, err_out, mse_out):
    tall = own_ref.shape[-1] // GROUP
    for i, out in enumerate((gd_ref, ge_ref)):
        sums = [[own_ref[i, t, k] + far_ref[i, t, k].astype(F32) for k in range(8)] for t in range(2)]
        for s in range(0, NSLOT, 2):
            pieces = []
            for n in (s, s + 1):
                xy, z = divmod(n, NZ)
                pieces.append(sums[0][z][:, xy * tall : (xy + 1) * tall])
                pieces.append(sums[1][xy][:, z * tall : (z + 1) * tall])
            out[:, s * 2 * tall : (s + 2) * 2 * tall] = jnp.concatenate(pieces, axis=1)
    err_out[...] = err_ref[...]
    mse_out[0, 0] = mse_ref[0, 0]


def local(inputs, dec_bias, enc_weight, enc_bias, dec_weight, other_recon, active_blocks):
    rows, width = inputs.shape
    tall = width // 2
    lats, features = dec_weight.shape
    share = lats // 4
    halves = (2, NSLOT, tall, rows)
    vmem = pl.BlockSpec(memory_space=pltpu.VMEM)
    hbm = pl.BlockSpec(memory_space=pl.ANY)
    dma = pltpu.SemaphoreType.DMA
    grad = (2, 2, 8, share, GROUP * tall)

    def coded(n):
        return pltpu.VMEM((2, n, tall, rows), jnp.int16), pltpu.VMEM((2, n, 1, 128), F32)

    error, mse, own, far = pl.pallas_call(
        kernel,
        name="sae_step",
        out_shape=(
            jax.ShapeDtypeStruct((width, rows), F32),
            jax.ShapeDtypeStruct((8, 128), F32),
            jax.ShapeDtypeStruct(grad, F32),
            jax.ShapeDtypeStruct(grad, BF16),
        ),
        in_specs=[vmem, vmem, hbm, vmem, hbm, vmem, vmem],
        out_specs=(vmem, vmem, hbm, hbm),
        scratch_shapes=[
            pltpu.VMEM((2, NSLOT, tall, lats), BF16),
            pltpu.VMEM(dec_weight.shape, BF16),
            pltpu.VMEM((2, NSLOT, tall, lats), BF16),
            pltpu.VMEM(halves, BF16),
            pltpu.VMEM(halves, BF16),
            pltpu.VMEM(halves, F32),
            *coded(NSLOT),
            *coded(NSLOT),
            *coded(2 * NZ),
            *coded(NZ),
            *coded(NZ),
            *coded(1),
            pltpu.VMEM((lats, rows), F32),
            pltpu.VMEM((lats, rows), BF16),
            pltpu.VMEM((lats, rows), F32),
            pltpu.VMEM((lats, rows), F32),
            pltpu.VMEM((2, 2, 8, 2, 2, share, GROUP * tall), F32),
            pltpu.VMEM((2, 2, 8, 2, share, GROUP * tall), F32),
            pltpu.VMEM(grad, BF16),
            pltpu.VMEM(grad, F32),
            pltpu.VMEM((NZ, 8, 128), F32),
            pltpu.VMEM((NX, 8, 128), F32),
            pltpu.VMEM((8, 8, 128), F32),
            pltpu.VMEM((3, 8, 128), F32),
            dma((3,)),
            dma((2,)),
            dma((2, NSLOT)),
            dma((2, 2)),
            dma((2, 2, NSLOT)),
            dma((2, 2, 2 * NZ)),
            dma((2, 2, NZ)),
            dma((2, 2, NZ)),
            dma((2, 2, 1)),
            dma((2,)),
            dma((2, NSLOT)),
            dma((2, 2, 8)),
            dma((2, 2, 8)),
            dma((2, 2, 8)),
            dma((2, 2, 8)),
            dma((2,)),
            dma((3,)),
            dma((3,)),
        ],
        compiler_params=pltpu.CompilerParams(
            collective_id=0, has_side_effects=True, vmem_limit_bytes=60 * 2**20
        ),
    )(
        inputs.T,
        dec_bias.reshape(1, -1),
        enc_weight.reshape(NSLOT, 2, tall, lats),
        enc_bias.reshape(1, -1),
        dec_weight,
        other_recon.T,
        active_blocks.T,
    )
    cut = 16
    part_spec = pl.BlockSpec((2, 2, 8, cut, GROUP * tall), lambda g: (0, 0, 0, g, 0))
    out_spec = pl.BlockSpec((cut, features), lambda g: (g, 0))
    err_spec = pl.BlockSpec((cut, rows), lambda g: (g, 0))
    scalar = pl.BlockSpec(memory_space=pltpu.SMEM)
    grad_dec, grad_enc, error, mse = pl.pallas_call(
        finish,
        name="finish",
        grid=(share // cut,),
        out_shape=(
            jax.ShapeDtypeStruct((share, features), F32),
            jax.ShapeDtypeStruct((share, features), F32),
            jax.ShapeDtypeStruct((width, rows), F32),
            jax.ShapeDtypeStruct((1, 1), F32),
        ),
        in_specs=[part_spec, part_spec, err_spec, scalar],
        out_specs=(out_spec, out_spec, err_spec, scalar),
    )(own, far, error, mse)
    return error.T, mse.reshape(()), grad_dec, grad_enc.T


def solution(mesh):
    placed = (
        P("dp", "lat"),
        P("lat"),
        P(None, "lat"),
        P("lat"),
        P("lat", None),
        P("dp", "lat"),
        P("dp", "lat"),
    )
    return jax.shard_map(
        local,
        mesh=mesh,
        in_specs=placed,
        out_specs=(P("dp", "lat"), P(), P(("lat", "dp"), None), P(None, ("lat", "dp"))),
        check_vma=False,
    )
```

time: 1100 us -> 142 us (0.13)
  waiting for transfers between devices: 780 us -> 0 us
  blocking collectives: 257 us -> 0 us
  Pallas kernels: 0 us -> 141 us
  matrix products: 25.9 us -> 0 us
  between operations: 16.3 us -> 0.64 us
  local copies, waits for them, and re-layouts: 15.4 us -> 0 us
    all_gather x2 -> x0, waiting for transfers between devices: 424 us -> none  [the longest x1 301 us: local(): lax.all_gather(error_local.astype(jnp.bfloat16), 'lat', axis=1, tiled=True)]
    unnamed x6 -> x0, waiting for transfers between devices: 325 us -> none
    pallas_call x0 -> x2, Pallas kernels: none -> 141 us  [the longest x1 137 us: local(): pl.pallas_call(kernel, name='sae_step', out_shape=(jax.ShapeDtypeStruct((...]
    unnamed x1 -> x0, blocking collectives: 140 us -> none
    psum x1 -> x0, blocking collectives: 118 us -> none  [local(): squares = lax.psum(jnp.sum(error_local * error_local), ('lat', 'dp'))]
    reduce_scatter x2 -> x0, waiting for transfers between devices: 31.1 us -> none  [the longest x1 31 us: local(): lax.psum_scatter(lax.dot_general(activations, error_bf, (((0,), (0,)), ((...]
    dot_general x4 -> x0, matrix products: 25.9 us -> none  [the longest x1 10.2 us: local(): lax.dot_general(centered, dpre, (((0,), (0,)), ((), ())), preferred_eleme...]
    unnamed x18 -> x0, local copies, waits for them, and re-layouts: 14 us -> none
  transfers between devices with their start and end apart: 5 -> 0, of which waited for: 4 -> 0; matrix products, arithmetic and copies ran while one was open for 1% -> 0% of each run, Pallas kernels for 0% -> 0%
where the time goes in v3:
time: 142 us
  Pallas kernels  141 us (99%)
    pallas_call x1, Pallas kernels, local(): pl.pallas_call(kernel, name='sae_step', out_shape=(jax.ShapeDtypeStruct((...  137 us
    pallas_call x1, Pallas kernels, local(): pl.pallas_call(finish, name='finish', grid=(share // cut,), out_shape=(ja...  4.69 us

profile of v3, /device:TPU:1, one launch (start us, length us, event | category | flops | bytes accessed | tf_op | source)
XLA Modules:
  0.0 142.0 jit_solution(2904198122684755260)
XLA Ops:
  0.6 136.7 %sae_step.1 = (f32[64,512]{1,0:T(8,128)}, f32[8,128]{1,0:T(8,128)}, f32[2,2,8,64,256]{4,3,2,1,0:T(8,128)}, bf16[2,2,8,64,256]{4,3,2,1,0:T(8,128)(2,1)}) custom-call(bf16[64,512]{1,0:T(8,128)(2,1)} %bitcast.11, bf16[1,64]{1,0:T(2,128)(2,1)} %bitcast.14, bf16[64,2,32,256]{3,2,1,0:T(8,128)(2,1)} %bitcast.9, f32[1,256]{1,0:T(1,128)} %bitcast.13, ...), custom_call_target="tpu_custom_call" | custom-call | tf_op jit(solution)/shard_map/sae_step/pallas_call | solution.py:575
  137.3 4.7 %finish.1 = (f32[64,4096]{1,0:T(8,128)}, f32[64,4096]{1,0:T(8,128)}, f32[64,512]{1,0:T(8,128)}, f32[1,1]{1,0:T(1,128)}) custom-call(f32[2,2,8,64,256]{4,3,2,1,0:T(8,128)} %get-tuple-element.12.own_ref, bf16[2,2,8,64,256]{4,3,2,1,0:T(8,128)(2,1)} %get-tuple-element.13.far_ref, f32[64,512]{1,0:T(8,128)} %get-tuple-element.14.err_ref, ...), custom_call_target="tpu_custom_call" | custom-call | tf_op jit(solution)/shard_map/finish/pallas_call | solution.py:647

commit v4 on v3

--- a/solution.py
+++ b/solution.py
@@ -300,31 +300,32 @@
             for _, slots in g.tree.chunks(b):
                 make(g.tree.t, slots)
 
+    make_all(q, 2)
     make_all(p, 4)
-    make_all(q, 2)
-    each(8, p.first, q.first)
+    each(8, q.first, lambda c: q.first(c + 8), p.first)
+    make_all(q, -1, 1)
     make_all(p, -3, 3)
-    each(8, lambda c: p.hop(3, c), lambda c: q.first(c + 8))
-    make_all(q, -1, 1)
+    each(8, lambda c: q.hop(1, c), lambda c: p.hop(3, c))
     make_all(p, -2, 2)
-    each(8, lambda c: p.hop(2, c), lambda c: q.hop(1, c))
+    each(8, lambda c: q.hop(1, c + 8), lambda c: p.hop(2, c))
+    make_all(q, 0)
     make_all(p, -1, 1, 0)
-    make_all(q, 0)
-    each(8, lambda c: p.hop(1, c), lambda c: q.hop(1, c + 8))
     q.to_y(4, -3, 3)
-    p.to_y(2, -1, 1)
+    each(4, lambda c: p.hop(1, c))
     q.ring_a(4)
     q.to_y(-2, 2)
-    p.ring_a(2)
+    each(4, lambda c: p.hop(1, c + 4))
     q.ring_a(3)
     q.to_y(-1, 1)
+    p.to_y(2, -1, 1)
+    q.ring_a(2)
+    q.to_y(0)
+    p.ring_a(2)
+    q.ring_a(1)
     p.to_y(0)
-    q.ring_a(2)
     p.ring_a(1)
-    q.to_y(0)
-    q.ring_a(1)
+    q.ring_a(0)
     p.ring_a(0)
-    q.ring_a(0)
     p.end()
     q.end()
 
@@ -639,7 +640,7 @@
         other_recon.T,
         active_blocks.T,
     )
-    cut = 16
+    cut = 32
     part_spec = pl.BlockSpec((2, 2, 8, cut, GROUP * tall), lambda g: (0, 0, 0, g, 0))
     out_spec = pl.BlockSpec((cut, features), lambda g: (g, 0))
     err_spec = pl.BlockSpec((cut, rows), lambda g: (g, 0))

time: 142 us -> 140 us (0.986)
  Pallas kernels: 141 us -> 139 us
    pallas_call x1, Pallas kernels: 137 us -> 135 us  [local(): pl.pallas_call(kernel, name='sae_step', out_shape=(jax.ShapeDtypeStruct((...]
where the time goes in v4:
time: 140 us
  Pallas kernels  139 us (99%)
    pallas_call x1, Pallas kernels, local(): pl.pallas_call(kernel, name='sae_step', out_shape=(jax.ShapeDtypeStruct((...  135 us
    pallas_call x1, Pallas kernels, local(): pl.pallas_call(finish, name='finish', grid=(share // cut,), out_shape=(ja...  4.08 us

profile of v4, /device:TPU:1, one launch (start us, length us, event | category | flops | bytes accessed | tf_op | source)
XLA Modules:
  0.0 139.8 jit_solution(2878078203556659318)
XLA Ops:
  0.6 135.1 %sae_step.1 = (f32[64,512]{1,0:T(8,128)}, f32[8,128]{1,0:T(8,128)}, f32[2,2,8,64,256]{4,3,2,1,0:T(8,128)}, bf16[2,2,8,64,256]{4,3,2,1,0:T(8,128)(2,1)}) custom-call(bf16[64,512]{1,0:T(8,128)(2,1)} %bitcast.11, bf16[1,64]{1,0:T(2,128)(2,1)} %bitcast.14, bf16[64,2,32,256]{3,2,1,0:T(8,128)(2,1)} %bitcast.9, f32[1,256]{1,0:T(1,128)} %bitcast.13, ...), custom_call_target="tpu_custom_call" | custom-call | tf_op jit(solution)/shard_map/sae_step/pallas_call | solution.py:576
  135.7 4.1 %finish.1 = (f32[64,4096]{1,0:T(8,128)}, f32[64,4096]{1,0:T(8,128)}, f32[64,512]{1,0:T(8,128)}, f32[1,1]{1,0:T(1,128)}) custom-call(f32[2,2,8,64,256]{4,3,2,1,0:T(8,128)} %get-tuple-element.12.own_ref, bf16[2,2,8,64,256]{4,3,2,1,0:T(8,128)(2,1)} %get-tuple-element.13.far_ref, f32[64,512]{1,0:T(8,128)} %get-tuple-element.14.err_ref, ...), custom_call_target="tpu_custom_call" | custom-call | tf_op jit(solution)/shard_map/finish/pallas_call | solution.py:648
